TPU v7x, 256 devices: a whole 4x4x8 slice. The times are simulated.
256 devices in a mesh: rep: 8 (over y, x_hi), blk: 32 (over z, x_lo, core).
Axes of the slice: x: 4 (x_hi: 2, x_lo: 2; x = x_hi * 2 + x_lo), y: 4, z: 8, core: 2. Of those that a mesh axis runs over, the one named last changes fastest.
Arguments:
- node_features: bfloat16 [65536, 256], P(('rep', 'blk')), may hold values from -6 to 6
- tile_values: bfloat16 [8, 32, 128, 128, 128], P('rep', 'blk'), may hold values from -0.09375 to 0.09375
- tile_row: int32 [8, 32, 128], P('rep', 'blk'), may hold values from 0 to 15, as said below
- tile_col: int32 [8, 32, 128], P('rep', 'blk'), may hold values from 0 to 63
- tile_count: int32 [8, 32], P('rep', 'blk'), may hold values from 16 to 128, as said below
- weight: bfloat16 [256, 256], replicated, may hold values from -0.375 to 0.375
- cotangent: bfloat16 [32, 8, 256, 256], P('blk', 'rep'), may hold values from -6 to 6
Outputs:
- layer_out: bfloat16 [32, 8, 256, 256], P('blk', 'rep')
- grad_weight: float32 [256, 256], replicated
- grad_features: bfloat16 [65536, 256], P(('rep', 'blk'))
Inputs may be any that keep to these rules, and one draw needn't show every extreme that they name: `tile_row`: within one device the live slots name distinct tile pairs. Slots 0 to tile_count - 1 of a device are live, the rest are ignored; some device has all 128 slots live.
All inputs are finite; a program needn't handle non-finite values.
Results may differ from a plain program's by a relative error of at most 0.03.
Values may be sent and summed in bfloat16 or wider, within the bound.
No kernel may reach another device: no remote copies, remote signals or barrier semaphores. Data moves between devices by JAX's collectives and lax.ppermute only.
A program may use at most 128 MiB of HBM per device.

v0:
```python
import jax
import jax.numpy as jnp
from jax import lax
from jax.sharding import PartitionSpec as P


def on_device(node_features, tile_values, tile_row, tile_col, tile_count, weight, cotangent):
    rows_dev, features = node_features.shape
    tile_block = tile_values[0, 0]
    slot_rows = tile_row[0, 0]
    slot_cols = tile_col[0, 0]
    live_count = tile_count[0, 0]
    slot_count = tile_block.shape[0]
    tile_size = tile_block.shape[1]
    rep_size = lax.axis_size("rep")
    slab_rows = rows_dev * rep_size
    slab_blocks = slab_rows // tile_size
    live_mask = (jnp.arange(slot_count, dtype=jnp.int32) < live_count).astype(jnp.float32)
    row_hot = (slot_rows[:, None] == jnp.arange(slab_blocks, dtype=jnp.int32)[None, :]).astype(
        jnp.float32
    ) * live_mask[:, None]
    gathered = lax.all_gather(node_features, "blk", axis=0, tiled=True)
    group_blocks = gathered.shape[0] // tile_size
    col_hot = (slot_cols[:, None] == jnp.arange(group_blocks, dtype=jnp.int32)[None, :]).astype(
        jnp.float32
    ) * live_mask[:, None]
    col_blocks = gathered.reshape(group_blocks, tile_size, features)
    picked = jnp.take(col_blocks, slot_cols, axis=0)
    products = jnp.einsum("tij,tjf->tif", tile_block, picked, preferred_element_type=jnp.float32)
    partial_value = (
        jnp.einsum("tk,tif->kif", row_hot, products)
        .reshape(slab_rows, features)
        .astype(jnp.bfloat16)
    )
    hidden_rows = (
        lax.psum_scatter(partial_value, "rep", scatter_dimension=0, tiled=True)
        .astype(jnp.float32)
        .astype(jnp.bfloat16)
    )
    preact = jnp.dot(hidden_rows, weight, preferred_element_type=jnp.float32)
    gating = jax.nn.sigmoid(preact)
    layer_out = (preact * gating).astype(jnp.bfloat16)
    slope_term = gating * (1.0 + preact * (1.0 - gating))
    grad_pre = (cotangent[0, 0].astype(jnp.float32) * slope_term).astype(jnp.bfloat16)
    weight_part = jnp.einsum("nf,ng->fg", hidden_rows, grad_pre, preferred_element_type=jnp.float32)
    grad_hidden = jnp.dot(grad_pre, weight.T, preferred_element_type=jnp.float32).astype(
        jnp.bfloat16
    )
    grad_slab = lax.all_gather(grad_hidden, "rep", axis=0, tiled=True)
    grad_weight = lax.psum(weight_part, ("rep", "blk"))
    grad_blocks = grad_slab.reshape(slab_blocks, tile_size, features)
    picked_rows = jnp.take(grad_blocks, slot_rows, axis=0)
    back_terms = jnp.einsum(
        "tij,tif->tjf", tile_block, picked_rows, preferred_element_type=jnp.float32
    )
    column_terms = (
        jnp.einsum("tk,tjf->kjf", col_hot, back_terms)
        .reshape(group_blocks * tile_size, features)
        .astype(jnp.bfloat16)
    )
    grad_features = (
        lax.psum_scatter(column_terms, "blk", scatter_dimension=0, tiled=True)
        .astype(jnp.float32)
        .astype(jnp.bfloat16)
    )
    return (layer_out.reshape(1, 1, rows_dev, features), grad_weight, grad_features)


def solution(mesh):
    placed = (
        P(("rep", "blk"), None),
        P("rep", "blk", None, None, None),
        P("rep", "blk", None),
        P("rep", "blk", None),
        P("rep", "blk"),
        P(),
        P("blk", "rep", None, None),
    )
    return jax.shard_map(
        on_device,
        mesh=mesh,
        in_specs=placed,
        out_specs=(P("blk", "rep", None, None), P(), P(("rep", "blk"), None)),
        check_vma=False,
    )
```

profile of v0, /device:TPU:24, one launch (start us, length us, event | category | flops | bytes accessed | tf_op | source)
XLA Modules:
  0.0 638.3 jit_solution(16897174415970150977)
XLA Ops:
  7.2 0.0 copy-start
  7.2 0.0 all-gather.3.cloned.1.call-start
  7.2 0.7 all-gather.3.cloned.1.call-update
  7.9 0.0 reduce-scatter.3.cloned.1.call-start
  8.6 0.7 fusion.32
  9.3 0.7 compare_and_fusion.1
  9.9 69.5 %all-gather.3.cloned.1.call-done = bf16[8192,256]{1,0:T(8,128)(2,1)} async-done(((bf16[256,256]{1,0:T(8,128)(2,1)}), bf16[8192,256]{1,0:T(8,128)(2,1)}) %all-gather.3.cloned.1.call-update) | async-done | bytes 4194320 | tf_op jit(solution)/shard_map/all_gather | solution.py:22
  79.4 8.8 %gather_fusion = bf16[128,128,256]{2,1,0:T(8,128)(2,1)} fusion(bf16[64,128,256]{2,1,0:T(8,128)(2,1)} %bitcast.51, s32[1024]{0:T(1024)S(1)} %pad_clamp_fusion.1), kind=kCustom, calls=%fused_computation | custom fusion | bytes 16777728 | tf_op jit(solution)/shard_map/jit(_take)/gather | solution.py:28
  88.2 11.9 %fusion.6 = bf16[128,256,128]{2,1,0:T(8,128)(2,1)} fusion(bf16[128,128,256]{2,1,0:T(8,128)(2,1)} %gather_fusion, pred[128]{0:T(512)(128)(4,1)S(1)} %compare_and_fusion.1, bf16[1,1,128,128,128]{4,3,2,1,0:T(8,128)(2,1)} %param.8), kind=kOutput, calls=%fused_computation.8 | convolution fusion | flops 1077936128 | bytes 20971648 | tf_op jit(solution)/shard_map/tij,tjf->tif/dot_general | solution.py:29
  100.1 0.0 copy-start.2
  100.1 12.4 %copy.12 = bf16[128,256,128]{1,0,2:T(8,128)(2,1)} copy(bf16[128,256,128]{2,1,0:T(8,128)(2,1)} %fusion.6) | data formatting | bytes 16777216 | tf_op jit(solution)/shard_map/tij,tjf->tif/dot_general | solution.py:29
  112.5 0.0 copy-start.4
  112.5 0.0 copy-done.2
  112.5 4.6 fusion.17
  117.1 1.4 copy.10
  118.4 0.0 reduce-scatter.3.cloned.1.call-update
  118.5 0.0 all-gather.5.cloned.1.call-start
  118.5 76.1 %reduce-scatter.3.cloned.1.call-done = bf16[256,256]{1,0:T(8,128)(2,1)} async-done(((bf16[2048,256]{1,0:T(8,128)(2,1)}), bf16[256,256]{1,0:T(8,128)(2,1)}) %reduce-scatter.3.cloned.1.call-update) | async-done | bytes 131088 | tf_op jit(solution)/shard_map/reduce_scatter | solution.py:36
  194.6 0.0 copy-done
  194.6 0.0 copy-done.4
  194.6 1.8 fusion.20
  196.5 0.9 convolution_convert_fusion
  197.4 0.0 all-gather.5.cloned.1.call-update
  197.4 0.0 all-reduce.2.cloned.1.call-start
  197.5 1.8 fusion.38
  199.3 0.0 all-reduce.2.cloned.1.call-update
  199.3 0.2 reduce-scatter.5.cloned.1.call-start
  199.6 49.1 %all-gather.5.cloned.1.call-done = bf16[2048,256]{1,0:T(8,128)(2,1)} async-done(((bf16[256,256]{1,0:T(8,128)(2,1)}), bf16[2048,256]{1,0:T(8,128)(2,1)}) %all-gather.5.cloned.1.call-update) | async-done | bytes 1048592 | tf_op jit(solution)/shard_map/all_gather | solution.py:49
  248.7 7.8 %gather_fusion.1 = bf16[128,128,256]{2,1,0:T(8,128)(2,1)} fusion(bf16[16,128,256]{2,1,0:T(8,128)(2,1)} %bitcast.50, s32[1024]{0:T(1024)S(1)} %pad_clamp_fusion), kind=kCustom, calls=%fused_computation.1 | custom fusion | bytes 16777728 | tf_op jit(solution)/shard_map/jit(_take)/gather | solution.py:52
  256.5 8.9 %fusion.4 = bf16[128,256,128]{2,1,0:T(8,128)(2,1)} fusion(bf16[128,128,256]{2,1,0:T(8,128)(2,1)} %gather_fusion.1, pred[128]{0:T(512)(128)(4,1)S(1)} %compare_and_fusion, bf16[1,1,128,128,128]{4,3,2,1,0:T(8,128)(2,1)} %param.8), kind=kOutput, calls=%fused_computation.6 | convolution fusion | flops 1077936128 | bytes 20971648 | tf_op jit(solution)/shard_map/tij,tif->tjf/dot_general | solution.py:53
  265.4 0.0 copy-start.3
  265.4 12.5 %copy.13 = bf16[128,256,128]{1,0,2:T(8,128)(2,1)} copy(bf16[128,256,128]{2,1,0:T(8,128)(2,1)} %fusion.4) | data formatting | bytes 16777216 | tf_op jit(solution)/shard_map/tij,tif->tjf/dot_general | solution.py:53
  277.8 0.0 copy-done.3
  277.8 0.0 copy-start.1
  277.8 4.7 fusion.14
  282.6 4.4 copy.11
  287.0 0.0 reduce-scatter.5.cloned.1.call-update
  287.0 217.9 %all-reduce.2.cloned.1.call-done = f32[256,256]{1,0:T(8,128)} async-done(((f32[256,256]{1,0:T(8,128)}), f32[256,256]{1,0:T(8,128)}) %all-reduce.2.cloned.1.call-update) | async-done | bytes 262160 | tf_op jit(solution)/shard_map/psum | solution.py:50
  504.9 125.2 %reduce-scatter.5.cloned.1.call-done = bf16[256,256]{1,0:T(8,128)(2,1)} async-done(((bf16[8192,256]{1,0:T(8,128)(2,1)}), bf16[256,256]{1,0:T(8,128)(2,1)}) %reduce-scatter.5.cloned.1.call-update) | async-done | bytes 131088 | tf_op jit(solution)/shard_map/reduce_scatter | solution.py:62
  630.1 1.7 copy.16
  631.7 0.0 copy-done.1
  (5 shorter events, 0.0 us)
Async XLA Ops:
  7.2 187.5 %copy-start = (bf16[256,256]{1,0:T(8,128)(2,1)S(1)}, bf16[256,256]{1,0:T(8,128)(2,1)}, u32[]{:S(2)}) copy-start(bf16[256,256]{1,0:T(8,128)(2,1)} %param.12) | copy-start | bytes 393220
  7.2 72.2 %all-gather.3.cloned.1.call-start = ((), (), s32[]{:S(2)}) async-start(), calls=%async_computation.2 | async-start | bytes 4325376 | tf_op jit(solution)/shard_map/all_gather | solution.py:22
  7.9 186.7 %reduce-scatter.3.cloned.1.call-start = ((), (), s32[]{:S(2)}) async-start(), calls=%async_computation.3 | async-start | bytes 1179648 | tf_op jit(solution)/shard_map/reduce_scatter | solution.py:36
  100.1 12.4 %copy-start.2 = (s32[1,1,128]{2,1,0:T(1,128)S(1)}, s32[1,1,128]{2,1,0:T(1,128)}, u32[]{:S(2)}) copy-start(s32[1,1,128]{2,1,0:T(1,128)} %param.9) | copy-start | bytes 1540
  112.5 82.2 %copy-start.4 = (bf16[1,1,256,256]{3,2,1,0:T(8,128)(2,1)S(1)}, bf16[1,1,256,256]{3,2,1,0:T(8,128)(2,1)}, u32[]{:S(2)}) copy-start(bf16[1,1,256,256]{3,2,1,0:T(8,128)(2,1)} %param.13) | copy-start | bytes 393220
  118.5 130.2 %all-gather.5.cloned.1.call-start = ((), (), s32[]{:S(2)}) async-start(), calls=%async_computation.5 | async-start | bytes 1179648 | tf_op jit(solution)/shard_map/all_gather | solution.py:49
  197.4 307.5 %all-reduce.2.cloned.1.call-start = ((), (), s32[]{:S(2)}) async-start(), calls=%async_computation.4 | async-start | bytes 524288 | tf_op jit(solution)/shard_map/psum | solution.py:50
  199.3 430.7 %reduce-scatter.5.cloned.1.call-start = ((), (), s32[]{:S(2)}) async-start(), calls=%async_computation.6 | async-start | bytes 4325376 | tf_op jit(solution)/shard_map/reduce_scatter | solution.py:62
  265.4 12.5 %copy-start.3 = (s32[1,1,128]{2,1,0:T(1,128)S(1)}, s32[1,1,128]{2,1,0:T(1,128)}, u32[]{:S(2)}) copy-start(s32[1,1,128]{2,1,0:T(1,128)} %param.10) | copy-start | bytes 1540
  277.8 353.9 %copy-start.1 = (bf16[256,256]{1,0:T(8,128)(2,1)S(1)}, bf16[256,256]{1,0:T(8,128)(2,1)}, u32[]{:S(2)}) copy-start(bf16[256,256]{1,0:T(8,128)(2,1)} %param.12) | copy-start | bytes 393220
Sparse Core Ops, SparseCore 0:
  9.9 69.5 all-gather.2
  118.6 76.0 reduce-scatter.2
  198.2 50.4 all-gather.4
  255.5 249.3 all-reduce.1
  508.0 122.0 reduce-scatter.4
where the time goes:
time: 639 us; the launch traced here: 638 us
  waiting for transfers between devices  539 us (84%)
  local copies, waits for them, and re-layouts  48.8 us (8%)
  matrix products  34.7 us (5%)
  between operations  14.5 us (2%)
    psum x1, waiting for transfers between devices, on_device(): grad_weight = lax.psum(weight_part, ('rep', 'blk'))  218 us
    reduce_scatter x1, waiting for transfers between devices, on_device(): lax.psum_scatter(column_terms, 'blk', scatter_dimension=0, tiled=True)  125 us
    reduce_scatter x1, waiting for transfers between devices, on_device(): lax.psum_scatter(partial_value, 'rep', scatter_dimension=0, tiled=True)  76.1 us
    all_gather x1, waiting for transfers between devices, on_device(): gathered = lax.all_gather(node_features, 'blk', axis=0, tiled=True)  69.5 us
    all_gather x1, waiting for transfers between devices, on_device(): grad_slab = lax.all_gather(grad_hidden, 'rep', axis=0, tiled=True)  49.1 us
  transfers between devices with their start and end apart: 5, of which 5 were waited for; matrix products, arithmetic and copies ran while one was open for 6% of the time, Pallas kernels for 0%

commit v1 on v0

--- a/solution.py
+++ b/solution.py
@@ -46,7 +46,9 @@
     grad_hidden = jnp.dot(grad_pre, weight.T, preferred_element_type=jnp.float32).astype(
         jnp.bfloat16
     )
-    grad_slab = lax.all_gather(grad_hidden, "rep", axis=0, tiled=True)
+    grad_slab = jnp.concatenate(
+        lax.all_to_all(jnp.stack([grad_hidden] * lax.axis_size("rep")), "rep", 0, 0), axis=0
+    )
     grad_weight = lax.psum(weight_part, ("rep", "blk"))
     grad_blocks = grad_slab.reshape(slab_blocks, tile_size, features)
     picked_rows = jnp.take(grad_blocks, slot_rows, axis=0)

time: 639 us -> 596 us (0.933)
  waiting for transfers between devices: 539 us -> 491 us
    all_gather x1 -> x0, waiting for transfers between devices: 49.1 us -> none  [on_device(): grad_slab = lax.all_gather(grad_hidden, 'rep', axis=0, tiled=True)]
    all_to_all x0 -> x1, waiting for transfers between devices: none -> 11 us  [on_device(): lax.all_to_all(jnp.stack([grad_hidden] * lax.axis_size('rep')), 'rep', 0, 0)]
    psum x1, waiting for transfers between devices: 218 us -> 209 us  [on_device(): grad_weight = lax.psum(weight_part, ('rep', 'blk'))]
  transfers between devices with their start and end apart: 5 -> 5, of which waited for: 5 -> 5; matrix products, arithmetic and copies ran while one was open for 6% -> 7% of each run, Pallas kernels for 0% -> 0%
where the time goes in v1:
time: 596 us; the launch traced here: 595 us
  waiting for transfers between devices  491 us (82%)
  local copies, waits for them, and re-layouts  48.9 us (8%)
  matrix products  33.9 us (6%)
  between operations  14.5 us (2%)
    psum x1, waiting for transfers between devices, on_device(): grad_weight = lax.psum(weight_part, ('rep', 'blk'))  209 us
    reduce_scatter x1, waiting for transfers between devices, on_device(): lax.psum_scatter(column_terms, 'blk', scatter_dimension=0, tiled=True)  125 us
    reduce_scatter x1, waiting for transfers between devices, on_device(): lax.psum_scatter(partial_value, 'rep', scatter_dimension=0, tiled=True)  76.1 us
    all_gather x1, waiting for transfers between devices, on_device(): gathered = lax.all_gather(node_features, 'blk', axis=0, tiled=True)  69.5 us
    dot_general x1, local copies, waits for them, and re-layouts, on_device(): jnp.einsum('tij,tif->tjf', tile_block, picked_rows, preferred_element_typ...  12.8 us
    dot_general x1, local copies, waits for them, and re-layouts, on_device(): jnp.einsum('tij,tjf->tif', tile_block, picked, preferred_element_type=jnp...  12.3 us
  transfers between devices with their start and end apart: 5, of which 5 were waited for; matrix products, arithmetic and copies ran while one was open for 7% of the time, Pallas kernels for 0%

profile of v1, /device:TPU:24, one launch (start us, length us, event | category | flops | bytes accessed | tf_op | source)
XLA Modules:
  0.0 595.0 jit_solution(171982931680560530)
XLA Ops:
  7.2 0.0 copy-start
  7.2 0.0 all-gather.2.cloned.1.call-start
  7.2 0.7 all-gather.2.cloned.1.call-update
  7.9 0.0 reduce-scatter.3.cloned.1.call-start
  8.6 0.7 fusion.32
  9.3 0.7 compare_and_fusion.1
  9.9 69.5 %all-gather.2.cloned.1.call-done = bf16[8192,256]{1,0:T(8,128)(2,1)} async-done(((bf16[256,256]{1,0:T(8,128)(2,1)}), bf16[8192,256]{1,0:T(8,128)(2,1)}) %all-gather.2.cloned.1.call-update) | async-done | bytes 4194320 | tf_op jit(solution)/shard_map/all_gather | solution.py:22
  79.4 8.8 %gather_fusion = bf16[128,128,256]{2,1,0:T(8,128)(2,1)} fusion(bf16[64,128,256]{2,1,0:T(8,128)(2,1)} %bitcast.51, s32[1024]{0:T(1024)S(1)} %pad_clamp_fusion.1), kind=kCustom, calls=%fused_computation | custom fusion | bytes 16777728 | tf_op jit(solution)/shard_map/jit(_take)/gather | solution.py:28
  88.2 11.8 %fusion.6 = bf16[128,256,128]{2,1,0:T(8,128)(2,1)} fusion(bf16[128,128,256]{2,1,0:T(8,128)(2,1)} %gather_fusion, pred[128]{0:T(512)(128)(4,1)S(1)} %compare_and_fusion.1, bf16[1,1,128,128,128]{4,3,2,1,0:T(8,128)(2,1)} %param.8), kind=kOutput, calls=%fused_computation.8 | convolution fusion | flops 1077936128 | bytes 20971648 | tf_op jit(solution)/shard_map/tij,tjf->tif/dot_general | solution.py:29
  100.0 0.0 copy-start.2
  100.0 12.3 %copy.12 = bf16[128,256,128]{1,0,2:T(8,128)(2,1)} copy(bf16[128,256,128]{2,1,0:T(8,128)(2,1)} %fusion.6) | data formatting | bytes 16777216 | tf_op jit(solution)/shard_map/tij,tjf->tif/dot_general | solution.py:29
  112.3 0.0 copy-start.4
  112.3 0.0 copy-done.2
  112.3 4.6 fusion.17
  116.9 1.4 copy.10
  118.2 0.0 reduce-scatter.3.cloned.1.call-update
  118.3 76.1 %reduce-scatter.3.cloned.1.call-done = bf16[256,256]{1,0:T(8,128)(2,1)} async-done(((bf16[2048,256]{1,0:T(8,128)(2,1)}), bf16[256,256]{1,0:T(8,128)(2,1)}) %reduce-scatter.3.cloned.1.call-update) | async-done | bytes 131088 | tf_op jit(solution)/shard_map/reduce_scatter | solution.py:36
  194.4 0.0 copy-done
  194.4 0.0 copy-done.4
  194.4 1.8 fusion.20
  196.2 0.2 convolution_convert_fusion
  196.5 1.0 stack.2
  197.5 5.4 all-to-all-start
  202.9 0.0 all-reduce.2.cloned.1.call-start
  202.9 1.8 fusion.38
  204.8 0.0 all-reduce.2.cloned.1.call-update
  204.8 0.2 reduce-scatter.5.cloned.1.call-start
  205.0 11.0 %all-to-all-done = bf16[8,256,256]{2,1,0:T(8,128)(2,1)S(1)} async-done(((bf16[8,256,256]{2,1,0:T(8,128)(2,1)}), bf16[8,256,256]{2,1,0:T(8,128)(2,1)S(1)}, u32[]{:S(2)}, u32[]{:S(2)}) %all-to-all-start) | async-done | bytes 1048608 | tf_op jit(solution)/shard_map/all_to_all | solution.py:50
  216.0 6.6 %gather_fusion.1 = bf16[128,128,256]{2,1,0:T(8,128)(2,1)} fusion(bf16[16,128,256]{2,1,0:T(8,128)(2,1)S(1)} %bitcast.50, s32[1024]{0:T(1024)S(1)} %pad_clamp_fusion), kind=kCustom, calls=%fused_computation.1 | custom fusion | bytes 16777728 | tf_op jit(solution)/shard_map/jit(_take)/gather | solution.py:54
  222.6 8.8 %fusion.4 = bf16[128,256,128]{2,1,0:T(8,128)(2,1)} fusion(bf16[128,128,256]{2,1,0:T(8,128)(2,1)} %gather_fusion.1, pred[128]{0:T(512)(128)(4,1)S(1)} %compare_and_fusion, bf16[1,1,128,128,128]{4,3,2,1,0:T(8,128)(2,1)} %param.8), kind=kOutput, calls=%fused_computation.6 | convolution fusion | flops 1077936128 | bytes 20971648 | tf_op jit(solution)/shard_map/tij,tif->tjf/dot_general | solution.py:55
  231.4 0.0 copy-start.3
  231.4 12.8 %copy.13 = bf16[128,256,128]{1,0,2:T(8,128)(2,1)} copy(bf16[128,256,128]{2,1,0:T(8,128)(2,1)} %fusion.4) | data formatting | bytes 16777216 | tf_op jit(solution)/shard_map/tij,tif->tjf/dot_general | solution.py:55
  244.3 0.0 copy-done.3
  244.3 0.0 copy-start.1
  244.3 4.7 fusion.14
  249.0 4.4 copy.11
  253.4 0.0 reduce-scatter.5.cloned.1.call-update
  253.4 208.6 %all-reduce.2.cloned.1.call-done = f32[256,256]{1,0:T(8,128)} async-done(((f32[256,256]{1,0:T(8,128)}), f32[256,256]{1,0:T(8,128)}) %all-reduce.2.cloned.1.call-update) | async-done | bytes 262160 | tf_op jit(solution)/shard_map/psum | solution.py:52
  462.0 124.8 %reduce-scatter.5.cloned.1.call-done = bf16[256,256]{1,0:T(8,128)(2,1)} async-done(((bf16[8192,256]{1,0:T(8,128)(2,1)}), bf16[256,256]{1,0:T(8,128)(2,1)}) %reduce-scatter.5.cloned.1.call-update) | async-done | bytes 131088 | tf_op jit(solution)/shard_map/reduce_scatter | solution.py:64
  586.8 1.7 copy.16
  588.5 0.0 copy-done.1
  (5 shorter events, 0.0 us)
Async XLA Ops:
  7.2 187.2 %copy-start = (bf16[256,256]{1,0:T(8,128)(2,1)S(1)}, bf16[256,256]{1,0:T(8,128)(2,1)}, u32[]{:S(2)}) copy-start(bf16[256,256]{1,0:T(8,128)(2,1)} %param.12) | copy-start | bytes 393220
  7.2 72.2 %all-gather.2.cloned.1.call-start = ((), (), s32[]{:S(2)}) async-start(), calls=%async_computation.3 | async-start | bytes 4325376 | tf_op jit(solution)/shard_map/all_gather | solution.py:22
  7.9 186.5 %reduce-scatter.3.cloned.1.call-start = ((), (), s32[]{:S(2)}) async-start(), calls=%async_computation.4 | async-start | bytes 1179648 | tf_op jit(solution)/shard_map/reduce_scatter | solution.py:36
  100.0 12.3 %copy-start.2 = (s32[1,1,128]{2,1,0:T(1,128)S(1)}, s32[1,1,128]{2,1,0:T(1,128)}, u32[]{:S(2)}) copy-start(s32[1,1,128]{2,1,0:T(1,128)} %param.9) | copy-start | bytes 1540
  112.3 82.1 %copy-start.4 = (bf16[1,1,256,256]{3,2,1,0:T(8,128)(2,1)S(1)}, bf16[1,1,256,256]{3,2,1,0:T(8,128)(2,1)}, u32[]{:S(2)}) copy-start(bf16[1,1,256,256]{3,2,1,0:T(8,128)(2,1)} %param.13) | copy-start | bytes 393220
  197.5 18.5 %all-to-all-start = ((bf16[8,256,256]{2,1,0:T(8,128)(2,1)}), bf16[8,256,256]{2,1,0:T(8,128)(2,1)S(1)}, u32[]{:S(2)}, u32[]{:S(2)}) async-start(bf16[8,256,256]{2,1,0:T(8,128)(2,1)} %stack.2), calls=%async_computation.1 | async-start | bytes 2097152 | tf_op jit(solution)/shard_map/all_to_all | solution.py:50
  202.9 259.2 %all-reduce.2.cloned.1.call-start = ((), (), s32[]{:S(2)}) async-start(), calls=%async_computation.5 | async-start | bytes 524288 | tf_op jit(solution)/shard_map/psum | solution.py:52
  204.8 382.1 %reduce-scatter.5.cloned.1.call-start = ((), (), s32[]{:S(2)}) async-start(), calls=%async_computation.6 | async-start | bytes 4325376 | tf_op jit(solution)/shard_map/reduce_scatter | solution.py:64
  231.4 12.8 %copy-start.3 = (s32[1,1,128]{2,1,0:T(1,128)S(1)}, s32[1,1,128]{2,1,0:T(1,128)}, u32[]{:S(2)}) copy-start(s32[1,1,128]{2,1,0:T(1,128)} %param.10) | copy-start | bytes 1540
  244.3 344.3 %copy-start.1 = (bf16[256,256]{1,0:T(8,128)(2,1)S(1)}, bf16[256,256]{1,0:T(8,128)(2,1)}, u32[]{:S(2)}) copy-start(bf16[256,256]{1,0:T(8,128)(2,1)} %param.12) | copy-start | bytes 393220
Sparse Core Ops, SparseCore 0:
  9.9 69.5 all-gather.1
  118.4 75.9 reduce-scatter.2
  210.6 251.3 all-reduce.1
  465.2 121.6 reduce-scatter.4
